TPU v7x, 256 devices: a whole 4x4x8 slice. The times are simulated.
256 devices in a mesh: lon: 16 (over x, y_lo, core), lat: 8 (over z), tm: 2 (over y_hi).
Axes of the slice: x: 4, y: 4 (y_hi: 2, y_lo: 2; y = y_hi * 2 + y_lo), z: 8, core: 2. Of those that a mesh axis runs over, the one named last changes fastest.
Arguments:
- snapshots: float32 [16, 8, 128, 2048], P('tm', None, 'lat', 'lon'), may hold values from -6 to 6
- basis: float32 [64, 8, 128, 2048], P(None, None, 'lat', 'lon'), may hold values from -6 to 6
Outputs:
- new_basis: float32 [64, 8, 128, 2048], P(None, None, 'lat', 'lon')
- coeffs: float32 [64, 16], P(None, 'tm')
All inputs are finite; a program needn't handle non-finite values.
Results may differ from a plain program's by a relative error of at most 0.00011.
Values sent between devices are 32-bit elements; how exact they have to be, the bound alone decides.
No kernel may reach another device: no remote copies, remote signals or barrier semaphores. Data moves between devices by JAX's collectives and lax.ppermute only.
A program may use at most 64 MiB of HBM per device.

v0:
```python
import math
import jax
import jax.numpy as jnp
from jax import lax
from jax.sharding import PartitionSpec as P

SMOOTH_RATE = 0.1
STEP_SIZE = 0.25


def with_halo(cells, sides, width, closed):
    for axis, dim in sides:
        count = lax.axis_size(axis)
        ends = count if closed else count - 1
        head = lax.slice_in_dim(cells, 0, width, axis=dim)
        tail = lax.slice_in_dim(cells, cells.shape[dim] - width, cells.shape[dim], axis=dim)
        cells = jnp.concatenate(
            [
                lax.ppermute(tail, axis, [(i, (i + 1) % count) for i in range(ends)]),
                cells,
                lax.ppermute(head, axis, [((i + 1) % count, i) for i in range(ends)]),
            ],
            axis=dim,
        )
    return cells


def product(left, right):
    return jnp.dot(left, right, precision=lax.Precision.HIGHEST, preferred_element_type=jnp.float32)


def laplace_step(extended):
    padded = jnp.pad(extended, ((0, 0), (1, 1), (0, 0), (0, 0)))
    center = extended[:, :, 1:-1, 1:-1]
    neighbours = padded[:, 2:, 1:-1, 1:-1] + padded[:, :-2, 1:-1, 1:-1]
    neighbours = neighbours + extended[:, :, 2:, 1:-1] + extended[:, :, :-2, 1:-1]
    neighbours = neighbours + extended[:, :, 1:-1, 2:] + extended[:, :, 1:-1, :-2]
    return center + SMOOTH_RATE * (neighbours - 6.0 * center)


def finish(grown, gram_matrix):
    factor = jnp.linalg.cholesky(gram_matrix)
    return jax.scipy.linalg.solve_triangular(factor, grown, lower=True)


def shards(snapshots, basis):
    snap_count, levels, rows_lat, cols_lon = snapshots.shape
    eof_count = basis.shape[0]
    total_cells = levels * rows_lat * cols_lon * lax.axis_size("lat") * lax.axis_size("lon")
    inv_root = 1.0 / math.sqrt(total_cells)
    smoothed = snapshots
    for sweep in range(3):
        lat_wide = with_halo(smoothed, (("lat", 2),), 1, False)
        extended = with_halo(lat_wide, (("lon", 3),), 1, True)
        smoothed = laplace_step(extended)
    flattened = smoothed.reshape(snap_count, -1)
    columns = basis.reshape(eof_count, -1)
    coeffs = lax.psum(product(columns, flattened.T), ("lon", "lat")) * inv_root
    update_term = STEP_SIZE * product(coeffs, flattened)
    grown = columns + lax.psum(update_term, "tm")
    gram_matrix = lax.psum(product(grown, grown.T), ("lon", "lat")) / total_cells
    new_basis = finish(grown, gram_matrix)
    return (new_basis.reshape(basis.shape), coeffs)


def solution(mesh):
    placed = (P("tm", None, "lat", "lon"), P(None, None, "lat", "lon"))
    return jax.shard_map(
        shards,
        mesh=mesh,
        in_specs=placed,
        out_specs=(P(None, None, "lat", "lon"), P(None, "tm")),
        check_vma=False,
    )
```

profile of v0, /device:TPU:16, one launch (start us, length us, event | category | flops | bytes accessed | tf_op | source)
XLA Modules:
  0.0 1095.1 jit_solution(14280274604795155072)
XLA Ops:
  9.7 4.5 collective-permute-start
  14.3 3.5 copy.78
  17.8 2.7 copy.79
  23.1 6.9 pad_maximum_fusion
  32.0 3.9 collective-permute-start.3
  35.9 2.9 copy.81
  41.6 3.8 collective-permute-start.4
  47.1 4.2 collective-permute-done.5
  55.6 4.3 collective-permute-done.6
  62.4 4.8 collective-permute-start.8
  68.8 4.3 collective-permute-done.9
  76.1 3.9 collective-permute-done.10
  83.8 5.3 fusion.7
  89.2 278.5 %psum.21 = f32[64,8]{0,1:T(8,128)S(1)} all-reduce(f32[64,8]{0,1:T(8,128)S(1)} %fusion.7), channel_id=1, replica_groups=mesh['lon'=16,'lat'=8,'tm'=2] {'lon','lat'}, use_global_device_ids=true, to_apply=%region_0.1 | all-reduce | flops 512 | bytes 4096 | tf_op jit(solution)/shard_map/psum | solution.py:58
  367.7 5.1 convolution_multiply_fusion
  372.8 112.3 %all-reduce.5.cloned.1.call-done = f32[64,16384]{1,0:T(8,128)} async-done(((f32[64,16384]{1,0:T(8,128)}), f32[64,16384]{1,0:T(8,128)}) %all-reduce.5.cloned.1.call-update) | async-done | bytes 4194320 | tf_op jit(solution)/shard_map/psum | solution.py:60
  485.1 14.0 %fusion.6 = f32[64,64]{0,1:T(8,128)S(1)} fusion(f32[64,16384]{1,0:T(8,128)} %all-reduce.5.cloned.1.call-done, f32[8,8,128,128]{3,2,1,0:T(8,128)} %bitcast.37), kind=kOutput, calls=%fused_computation.21 | convolution fusion | flops 806354944 | bytes 8404992 | tf_op jit(solution)/shard_map/dot_general | solution.py:29
  499.1 555.0 %psum.23 = f32[64,64]{0,1:T(8,128)S(1)} all-reduce(f32[64,64]{0,1:T(8,128)S(1)} %fusion.6), channel_id=1, replica_groups=mesh['lon'=16,'lat'=8,'tm'=2] {'lon','lat'}, use_global_device_ids=true, to_apply=%region_2.3 | all-reduce | flops 4096 | bytes 32768 | tf_op jit(solution)/shard_map/psum | solution.py:61
  1054.1 6.1 fusion.5
  1060.2 2.8 copy.121
  1063.1 5.8 cholesky.16
  1070.3 4.9 custom-call.7
  1075.2 8.4 fusion
  1083.6 4.4 copy.110
  (58 shorter events, 28.1 us)
Async XLA Ops:
  7.2 477.9 %all-reduce.5.cloned.1.call-start = ((), (), s32[]{:S(2)}) async-start(), calls=%async_computation | async-start | bytes 8388608 | tf_op jit(solution)/shard_map/psum | solution.py:60
  8.4 9.4 collective-permute-start.1
  9.7 10.7 collective-permute-start
  30.0 2.0 copy-start.1
  32.0 6.7 collective-permute-start.2
  32.0 7.2 collective-permute-start.3
  41.6 5.4 collective-permute-start.4
  45.5 5.8 collective-permute-start.5
  52.0 3.1 collective-permute-start.7
  54.0 6.0 collective-permute-start.6
  62.4 6.4 collective-permute-start.8
  67.3 5.9 collective-permute-start.9
  73.9 1.7 collective-permute-start.11
  74.5 5.5 collective-permute-start.10
  81.6 2.2 copy-start
  367.7 5.1 copy-start.2
Sparse Core Ops, SparseCore 0:
  372.9 112.1 all-reduce.4
where the time goes:
time: 1100 us
  blocking collectives  834 us (76%)
  waiting for transfers between devices  131 us (12%)
  matrix products  32.8 us (3%)
  other arithmetic  30.9 us (3%)
  local copies, waits for them, and re-layouts  29 us (3%)
  starting transfers between devices  23.6 us (2%)
  between operations  14.5 us (1%)
    psum x1, blocking collectives, shards(): lax.psum(product(grown, grown.T), ('lon', 'lat')) / total_cells  555 us
    psum x1, blocking collectives, shards(): coeffs = lax.psum(product(columns, flattened.T), ('lon', 'lat')) * inv_root  279 us
    psum x1, waiting for transfers between devices, shards(): grown = columns + lax.psum(update_term, 'tm')  112 us
    dot_general x3, matrix products, product(): jnp.dot(left, right, precision=lax.Precision.HIGHEST, preferred_element_t...  24.4 us
  transfers between devices with their start and end apart: 13, of which 9 were waited for; matrix products, arithmetic and copies ran while one was open for 1% of the time, Pallas kernels for 0%

commit v1 on v0

--- a/solution.py
+++ b/solution.py
@@ -55,7 +55,7 @@
         smoothed = laplace_step(extended)
     flattened = smoothed.reshape(snap_count, -1)
     columns = basis.reshape(eof_count, -1)
-    coeffs = lax.psum(product(columns, flattened.T), ("lon", "lat")) * inv_root
+    coeffs = lax.psum(lax.psum(product(columns, flattened.T), "lon"), "lat") * inv_root
     update_term = STEP_SIZE * product(coeffs, flattened)
     grown = columns + lax.psum(update_term, "tm")
     gram_matrix = lax.psum(product(grown, grown.T), ("lon", "lat")) / total_cells

time: 1100 us -> 873 us (0.79)
  blocking collectives: 834 us -> 599 us
    psum x1 -> x2, blocking collectives: 279 us -> 44.2 us  [the longest x1 27.1 us: shards(): lax.psum(product(columns, flattened.T), 'lon')]
where the time goes in v1:
time: 873 us; the launch traced here: 865 us
  blocking collectives  599 us (69%)
  waiting for transfers between devices  135 us (15%)
  matrix products  32.8 us (4%)
  other arithmetic  31 us (4%)
  local copies, waits for them, and re-layouts  29 us (3%)
  starting transfers between devices  23.6 us (3%)
  between operations  14.5 us (2%)
    psum x1, blocking collectives, shards(): lax.psum(product(grown, grown.T), ('lon', 'lat')) / total_cells  555 us
    psum x1, waiting for transfers between devices, shards(): grown = columns + lax.psum(update_term, 'tm')  117 us
    psum x1, blocking collectives, shards(): lax.psum(product(columns, flattened.T), 'lon')  27.1 us
    dot_general x3, matrix products, product(): jnp.dot(left, right, precision=lax.Precision.HIGHEST, preferred_element_t...  24.3 us
  transfers between devices with their start and end apart: 13, of which 9 were waited for; matrix products, arithmetic and copies ran while one was open for 1% of the time, Pallas kernels for 0%

profile of v1, /device:TPU:16, one launch (start us, length us, event | category | flops | bytes accessed | tf_op | source)
XLA Modules:
  0.0 865.1 jit_solution(14600010781492581711)
XLA Ops:
  9.7 4.5 collective-permute-start
  14.3 3.5 copy.78
  23.1 6.9 pad_maximum_fusion
  32.0 3.9 collective-permute-start.3
  35.9 2.9 copy.81
  41.6 3.8 collective-permute-start.4
  47.0 4.2 collective-permute-done.5
  55.6 4.3 collective-permute-done.6
  62.4 4.8 collective-permute-start.8
  68.8 4.3 collective-permute-done.9
  76.1 3.9 collective-permute-done.10
  83.8 5.3 fusion.7
  89.2 27.1 %psum.28 = f32[64,8]{0,1:T(8,128)S(1)} all-reduce(f32[64,8]{0,1:T(8,128)S(1)} %fusion.7), channel_id=1, replica_groups=mesh['lon'=16,'lat'=8,'tm'=2] {'lon'}, use_global_device_ids=true, to_apply=%region_0.1 | all-reduce | flops 512 | bytes 4096 | tf_op jit(solution)/shard_map/psum | solution.py:58
  116.3 17.1 %psum.29 = f32[64,8]{0,1:T(8,128)S(1)} all-reduce(f32[64,8]{0,1:T(8,128)S(1)} %psum.28), channel_id=1, replica_groups=mesh['lon'=16,'lat'=8,'tm'=2] {'lat'}, use_global_device_ids=true, to_apply=%region_1.2 | all-reduce | flops 512 | bytes 4096 | tf_op jit(solution)/shard_map/psum | solution.py:58
  133.4 5.1 convolution_multiply_fusion
  138.5 116.5 %all-reduce.5.cloned.1.call-done = f32[64,16384]{1,0:T(8,128)} async-done(((f32[64,16384]{1,0:T(8,128)}), f32[64,16384]{1,0:T(8,128)}) %all-reduce.5.cloned.1.call-update) | async-done | bytes 4194320 | tf_op jit(solution)/shard_map/psum | solution.py:60
  255.0 13.9 %fusion.6 = f32[64,64]{0,1:T(8,128)S(1)} fusion(f32[64,16384]{1,0:T(8,128)} %all-reduce.5.cloned.1.call-done, f32[8,8,128,128]{3,2,1,0:T(8,128)} %bitcast.37), kind=kOutput, calls=%fused_computation.21 | convolution fusion | flops 806354944 | bytes 8404992 | tf_op jit(solution)/shard_map/dot_general | solution.py:29
  269.0 555.0 %psum.31 = f32[64,64]{0,1:T(8,128)S(1)} all-reduce(f32[64,64]{0,1:T(8,128)S(1)} %fusion.6), channel_id=1, replica_groups=mesh['lon'=16,'lat'=8,'tm'=2] {'lon','lat'}, use_global_device_ids=true, to_apply=%region_3.4 | all-reduce | flops 4096 | bytes 32768 | tf_op jit(solution)/shard_map/psum | solution.py:61
  824.0 6.1 fusion.5
  830.1 2.8 copy.121
  833.0 5.8 cholesky.16
  840.3 4.9 custom-call.7
  845.2 8.4 fusion
  853.6 4.4 copy.110
  (59 shorter events, 30.9 us)
Async XLA Ops:
  7.2 247.9 %all-reduce.5.cloned.1.call-start = ((), (), s32[]{:S(2)}) async-start(), calls=%async_computation | async-start | bytes 8388608 | tf_op jit(solution)/shard_map/psum | solution.py:60
  8.4 9.4 %collective-permute-start.1 = (f32[8,8,1,128]{3,1,2,0:T(8,128)S(1)}, f32[8,8,1,128]{3,1,2,0:T(8,128)S(1)}, u32[]{:S(2)}, u32[]{:S(2)}) collective-permute-start(f32[8,8,1,128]{3,1,2,0:T(8,128)S(1)} %get-tuple-element.23), channel_id=1, source_target_pairs={{2,0},{4,2},{6,4},{8,6},{10,8},{12,10},{14,12},{3,1},{5,3},{7,5},{... | collective-permute-start | bytes 98312 | tf_op jit(solution)/shard_map/ppermute | solution.py:21
  9.7 10.7 %collective-permute-start = (f32[8,8,1,128]{3,1,2,0:T(8,128)S(1)}, f32[8,8,1,128]{3,1,2,0:T(8,128)S(1)}, u32[]{:S(2)}, u32[]{:S(2)}) collective-permute-start(f32[8,8,1,128]{3,1,2,0:T(8,128)S(1)} %get-tuple-element.22), channel_id=1, source_target_pairs={{0,2},{2,4},{4,6},{6,8},{8,10},{10,12},{12,14},{1,3},{3,5},{5,7},{... | collective-permute-start | bytes 98312 | tf_op jit(solution)/shard_map/ppermute | solution.py:19
  30.0 2.0 copy-start.1
  32.0 6.7 collective-permute-start.2
  32.0 7.2 collective-permute-start.3
  41.6 5.4 collective-permute-start.4
  45.5 5.8 collective-permute-start.5
  52.0 3.1 collective-permute-start.7
  54.0 6.0 collective-permute-start.6
  62.4 6.4 collective-permute-start.8
  67.3 5.9 collective-permute-start.9
  73.9 1.7 collective-permute-start.11
  74.5 5.5 collective-permute-start.10
  81.6 2.2 copy-start
  133.4 5.1 copy-start.2
Sparse Core Ops, SparseCore 0:
  138.6 116.3 all-reduce.4
